TPU v7x, 32 devices: a whole 2x2x4 slice. The times are simulated.
32 devices in a mesh: group: 2 (over y), frame: 16 (over z, x, core).
Axes of the slice: x: 2, y: 2, z: 4, core: 2. Of those that a mesh axis runs over, the one named last changes fastest.
Arguments:
- queries: bfloat16 [8192, 1536], P(('group', 'frame')), parts along dimension 0, may hold values from -120 to 120, as said below
- key_rows: bfloat16 [8192, 1536], P(('group', 'frame')), parts along dimension 0, may hold values from -6 to 6, as said below
- value_rows: bfloat16 [8192, 1536], P(('group', 'frame')), parts along dimension 0, may hold values from -6 to 6
- out_grad: bfloat16 [8192, 1536], P(('group', 'frame')), parts along dimension 0, may hold values from -6 to 6
- block_mask: int32 [32, 4, 2], P(('group', 'frame')), parts along dimension 0, may hold values 0 or 1
- block_pick: int32 [32, 4], P(('group', 'frame')), parts along dimension 0, may hold values from 0 to 1
Outputs:
- attended: bfloat16 [8192, 1536], P(('group', 'frame')), parts along dimension 0
- query_grad: bfloat16 [8192, 1536], P(('group', 'frame')), parts along dimension 0
- key_grad: bfloat16 [8192, 1536], P(('group', 'frame')), parts along dimension 0
- value_grad: bfloat16 [8192, 1536], P(('group', 'frame')), parts along dimension 0
There are 2 independent parts, one for each index of `group`. A program takes and returns all parts, laid end to end along the dimension named above; each array names one. Nothing has to cross between parts.
Inputs may be any that keep to these rules, and one draw needn't show every extreme that they name: queries of order one; in some draws a few rows are strongly aligned with the keys of two consecutive rows. `key_rows`: keys of order one.
All inputs are finite; a program needn't handle non-finite values. No bound on the sum of `block_mask` on one device may be relied on, other than what follows from the above.
Results may differ from a plain program's by a relative error of at most 0.0054.
Values may be sent and summed in bfloat16 or wider, within the bound.
No kernel may reach another device: no remote copies, remote signals or barrier semaphores. Data moves between devices by JAX's collectives and lax.ppermute only.
A program may use at most 128 MiB of HBM per device.

v0:
```python
import jax
import jax.numpy as jnp
from jax import lax
from jax.sharding import PartitionSpec as P

HEADS = 12
HDIM = 128
BLK = 128
EDGE = 64


def padded(block, sides, width):
    for axis, dim in sides:
        count = lax.axis_size(axis)
        forward = [(i, i + 1) for i in range(count - 1)]
        backward = [(target, source) for source, target in forward]
        low = lax.ppermute(
            lax.slice_in_dim(block, block.shape[dim] - width, None, axis=dim), axis, forward
        )
        high = lax.ppermute(lax.slice_in_dim(block, 0, width, axis=dim), axis, backward)
        block = jnp.concatenate([low, block, high], axis=dim)
    return block


def partner(value, axis, bit):
    mask = 2**bit
    pairs = [(source, source ^ mask) for source in range(lax.axis_size(axis))]
    return lax.ppermute(value, axis, pairs)


def shifted(value, axis, steps):
    count = lax.axis_size(axis)
    initial, last = (max(0, -steps), min(count, count - steps))
    return lax.ppermute(value, axis, [(source, source + steps) for source in range(initial, last)])


def split_heads(rows_blk):
    return rows_blk.reshape(rows_blk.shape[0], HEADS, HDIM)


def score_block(query_blk, key_blk, valid):
    scores = jnp.einsum(
        "qhd,khd->hqk",
        split_heads(query_blk),
        split_heads(key_blk),
        preferred_element_type=jnp.float32,
    ) * HDIM ** (-0.5)
    return jnp.where(valid[None], scores, -jnp.inf)


def forward_part(query_blk, key_blk, value_blk, valid):
    scores = score_block(query_blk, key_blk, valid)
    highest = jnp.max(scores, axis=2, keepdims=True)
    weights = jnp.exp(scores - highest)
    totals = jnp.sum(weights, axis=2, keepdims=True)
    weights = weights / totals
    rounded = weights.astype(jnp.bfloat16)
    attended = jnp.einsum(
        "hqk,khd->qhd", rounded, split_heads(value_blk), preferred_element_type=jnp.float32
    )
    attended = attended.astype(jnp.bfloat16).reshape(query_blk.shape[0], -1)
    return (attended, weights, rounded, highest, totals)


def backward_part(query_blk, grad_blk, key_blk, value_blk, weights, rounded):
    scale = HDIM ** (-0.5)
    grad_h = split_heads(grad_blk)
    dprob = jnp.einsum(
        "qhd,khd->hqk", grad_h, split_heads(value_blk), preferred_element_type=jnp.float32
    )
    inner = jnp.sum(weights * dprob, axis=2, keepdims=True)
    dscore = (weights * (dprob - inner)).astype(jnp.bfloat16)
    query_grad = (
        jnp.einsum("hqk,khd->qhd", dscore, split_heads(key_blk), preferred_element_type=jnp.float32)
        * scale
    )
    query_grad = query_grad.astype(jnp.bfloat16).reshape(query_blk.shape[0], -1)
    key_term = (
        jnp.einsum(
            "hqk,qhd->khd", dscore, split_heads(query_blk), preferred_element_type=jnp.float32
        )
        * scale
    )
    value_term = jnp.einsum("hqk,qhd->khd", rounded, grad_h, preferred_element_type=jnp.float32)
    count = key_blk.shape[0]
    return (query_grad, jnp.stack([key_term.reshape(count, -1), value_term.reshape(count, -1)]))


def fetch_keys(stacked, picks, levels, again):
    if again:
        extended = padded(stacked, (("frame", 1),), EDGE)
    else:
        extended = padded(stacked, (("frame", 1),), EDGE)
    pieces = [extended]
    for bit_level in range(levels):
        start = picks[bit_level] * BLK
        piece = lax.dynamic_slice_in_dim(stacked, start, BLK, 1)
        if again:
            pieces.append(partner(piece, "frame", bit_level))
        else:
            pieces.append(partner(piece, "frame", bit_level))
    return jnp.concatenate(pieces, axis=1)


def send_edge(terms, offset):
    return shifted(terms, "frame", offset)


def per_device(queries, key_rows, value_rows, out_grad, block_mask, block_pick):
    frames = lax.axis_size("frame")
    levels = frames.bit_length() - 1
    device = lax.axis_index("frame")
    tokens = queries.shape[0]
    blocks = tokens // BLK
    picks = block_pick[0]
    stacked = jnp.stack([key_rows, value_rows])
    row_block = jnp.arange(tokens, dtype=jnp.int32) // BLK
    onehot = row_block[:, None] == jnp.arange(blocks, dtype=jnp.int32)[None, :]
    chosen = jnp.sum(jnp.where(onehot[None], block_mask[0][:, None, :], 0), axis=2)
    panel_ok = jnp.broadcast_to((chosen > 0).T[:, :, None], (tokens, levels, BLK)).reshape(
        tokens, levels * BLK
    )
    valid = jnp.concatenate(
        [
            jnp.broadcast_to(device > 0, (tokens, EDGE)),
            jnp.ones((tokens, tokens), bool),
            jnp.broadcast_to(device < frames - 1, (tokens, EDGE)),
            panel_ok,
        ],
        axis=1,
    )
    gathered = fetch_keys(stacked, picks, levels, False)
    attended, weights, rounded, highest, totals = forward_part(
        queries, gathered[0], gathered[1], valid
    )
    fetched = fetch_keys(stacked, picks, levels, True)
    scores = score_block(queries, fetched[0], valid)
    weights = jnp.exp(scores - highest) / totals
    rounded = weights.astype(jnp.bfloat16)
    query_grad, terms = backward_part(queries, out_grad, fetched[0], fetched[1], weights, rounded)
    own = terms[:, EDGE : EDGE + tokens]
    from_above = send_edge(terms[:, :EDGE].astype(jnp.bfloat16), -1)
    own = own.at[:, tokens - EDGE :].add(from_above.astype(jnp.float32))
    from_below = send_edge(terms[:, EDGE + tokens : 2 * EDGE + tokens].astype(jnp.bfloat16), 1)
    own = own.at[:, :EDGE].add(from_below.astype(jnp.float32))
    first = 2 * EDGE + tokens
    for bit_level in range(levels):
        piece = terms[:, first + bit_level * BLK : first + (bit_level + 1) * BLK].astype(
            jnp.bfloat16
        )
        returned = partner(piece, "frame", bit_level)
        start = picks[bit_level] * BLK
        current = lax.dynamic_slice_in_dim(own, start, BLK, 1)
        own = lax.dynamic_update_slice_in_dim(own, current + returned.astype(jnp.float32), start, 1)
    return (attended, query_grad, own[0].astype(jnp.bfloat16), own[1].astype(jnp.bfloat16))


def solution(mesh):
    return jax.shard_map(
        per_device,
        mesh=mesh,
        in_specs=(
            P(("group", "frame"), None),
            P(("group", "frame"), None),
            P(("group", "frame"), None),
            P(("group", "frame"), None),
            P(("group", "frame"), None, None),
            P(("group", "frame"), None),
        ),
        out_specs=(
            P(("group", "frame"), None),
            P(("group", "frame"), None),
            P(("group", "frame"), None),
            P(("group", "frame"), None),
        ),
        check_vma=False,
    )
```

profile of v0, /device:TPU:0, one launch (start us, length us, event | category | flops | bytes accessed | tf_op | source)
XLA Modules:
  0.0 190.3 jit_solution(15812177975088462882)
XLA Ops:
  4.8 2.5 %collective-permute-start = (bf16[2,64,1536]{2,1,0:T(8,128)(2,1)}, bf16[2,64,1536]{2,1,0:T(8,128)(2,1)S(1)}, u32[]{:S(2)}, u32[]{:S(2)}) collective-permute-start(bf16[2,64,1536]{2,1,0:T(8,128)(2,1)} %copy.66), channel_id=1, source_target_pairs={{0,1},{1,2},{2,3},{3,4},{4,5},{5,6},{6,7},{7,8},{8,9},{9,10},{10,1... | collective-permute-start | bytes 1179656 | tf_op jit(solution)/shard_map/ppermute | solution.py:17
  10.5 2.0 %fusion.22 = (bf16[2,128,1536]{1,2,0:T(8,128)(2,1)}, bf16[2,128,1536]{1,2,0:T(8,128)(2,1)}, bf16[2,128,1536]{1,2,0:T(8,128)(2,1)}, bf16[2,128,1536]{1,2,0:T(8,128)(2,1)}) fusion(s32[]{:T(128)S(6)} %select_n.45, bf16[1,256,1536]{1,2,0:T(8,128)(2,1)S(1)} %bitcast.72, bf16[1,256,1536]{1,2,0:T(8,128)(2,1)S(1)} %bitcast.75, s32[]{:T(128)S(6)} %select_n.42, ...), kind=kLoop, calls=%fused_computation.50 | loop fusion | flops 6291456 | bytes 4718608 | tf_op jit(solution)/shard_map/stack | solution.py:116
  12.5 2.6 %collective-permute-start.2 = (bf16[2,128,1536]{1,2,0:T(8,128)(2,1)}, bf16[2,128,1536]{1,2,0:T(8,128)(2,1)}, u32[]{:S(2)}, u32[]{:S(2)}) collective-permute-start(bf16[2,128,1536]{1,2,0:T(8,128)(2,1)} %get-tuple-element.55), channel_id=1, source_target_pairs={{0,1},{1,0},{2,3},{3,2},{4,5},{5,4},{6,7},{7,6},{8,9},{9,8},{10,11... | collective-permute-start | bytes 2359304 | tf_op jit(solution)/shard_map/ppermute | solution.py:28
  15.1 1.5 collective-permute-start.3
  16.6 1.6 collective-permute-start.4
  21.7 2.3 %copy.74 = bf16[256,1536]{0,1:T(8,128)(2,1)} copy(bf16[256,1536]{1,0:T(8,128)(2,1)} %param.13) | data formatting | bytes 1572864 | tf_op args[3]
  24.0 1.5 collective-permute-start.1
  29.3 5.5 %collective-permute-done.3 = bf16[2,128,1536]{1,2,0:T(8,128)(2,1)} collective-permute-done((bf16[2,128,1536]{1,2,0:T(8,128)(2,1)}, bf16[2,128,1536]{1,2,0:T(8,128)(2,1)}, u32[]{:S(2)}, u32[]{:S(2)}) %collective-permute-start.3) | collective-permute-done | bytes 786464 | tf_op jit(solution)/shard_map/ppermute | solution.py:28
  34.8 18.0 %collective-permute-done.4 = bf16[2,128,1536]{1,2,0:T(8,128)(2,1)} collective-permute-done((bf16[2,128,1536]{1,2,0:T(8,128)(2,1)}, bf16[2,128,1536]{1,2,0:T(8,128)(2,1)}, u32[]{:S(2)}, u32[]{:S(2)}) %collective-permute-start.4) | collective-permute-done | bytes 786464 | tf_op jit(solution)/shard_map/ppermute | solution.py:28
  52.8 2.5 %collective-permute-done.5 = bf16[2,128,1536]{1,2,0:T(8,128)(2,1)} collective-permute-done((bf16[2,128,1536]{1,2,0:T(8,128)(2,1)}, bf16[2,128,1536]{1,2,0:T(8,128)(2,1)}, u32[]{:S(2)}, u32[]{:S(2)}) %collective-permute-start.5) | collective-permute-done | bytes 786464 | tf_op jit(solution)/shard_map/ppermute | solution.py:28
  55.3 9.2 %concatenate.11 = bf16[2,896,1536]{1,2,0:T(8,128)(2,1)} concatenate(bf16[2,64,1536]{1,2,0:T(8,128)(2,1)S(1)} %copy.68, bf16[2,256,1536]{1,2,0:T(8,128)(2,1)S(1)} %pad_maximum_fusion.1, bf16[2,64,1536]{1,2,0:T(8,128)(2,1)S(1)} %copy.69, bf16[2,128,1536]{1,2,0:T(8,128)(2,1)} %collective-permute-done.2, bf16[2,128,1536]{1,2,0:T(8,128)(2,1)} %collective-permute-done.3, ...), dimensions={1} | concatenate | bytes 11010048 | tf_op jit(solution)/shard_map/concatenate | solution.py:102
  64.5 4.7 %fusion.33 = (bf16[1,896,1536]{1,2,0:T(8,128)(2,1)S(1)}, bf16[1,896,1536]{1,2,0:T(8,128)(2,1)}) fusion(bf16[2,896,1536]{1,2,0:T(8,128)(2,1)} %concatenate.11), kind=kLoop, calls=%fused_computation.71 | loop fusion | bytes 11010048 | tf_op jit(solution)/shard_map/slice | solution.py:134
  69.3 7.6 %fusion.35 = (f32[12,256]{1,0:T(8,128)S(1)}, f32[12,256,896]{1,2,0:T(8,128)}) fusion(pred[256,896]{0,1:T(8,128)(4,1)} %pad_add_fusion, bf16[896,12,128]{0,2,1:T(8,128)(2,1)S(1)} %bitcast.68, bf16[256,12,128]{0,2,1:T(8,128)(2,1)S(1)} %bitcast.79), kind=kOutput, calls=%fused_computation.73 | convolution fusion | flops 715654016 | bytes 14790656 | tf_op jit(solution)/shard_map/sub | solution.py:54
  76.9 7.0 %fusion.14 = bf16[12,128,256]{2,1,0:T(8,128)(2,1)} fusion(bf16[896,12,128]{0,2,1:T(8,128)(2,1)} %bitcast.81, f32[12,256,896]{1,2,0:T(8,128)} %get-tuple-element.65, f32[12,256]{1,0:T(8,128)S(1)} %get-tuple-element.64), kind=kOutput, calls=%fused_computation.43 | convolution fusion | flops 710541312 | bytes 14561280 | tf_op jit(solution)/shard_map/hqk,khd->qhd/dot_general | solution.py:58
  86.2 5.2 %fusion.2 = (f32[12,256]{1,0:T(8,128)S(1)}, f32[12,896,256]{2,1,0:T(8,128)}) fusion(f32[12,256,896]{1,2,0:T(8,128)S(1)} %copy-done.3, f32[12,256]{1,0:T(8,128)S(1)} %get-tuple-element.64, bf16[896,12,128]{0,2,1:T(8,128)(2,1)S(1)} %bitcast.82, bf16[256,12,128]{0,2,1:T(8,128)(2,1)S(1)} %bitcast.83), kind=kOutput, calls=%fused_computation.9 | convolution fusion | flops 712897536 | bytes 25583616 | tf_op jit(solution)/shard_map/qhd,khd->hqk/dot_general | solution.py:68
  91.4 4.1 %fusion.10 = f32[12,896,128]{1,2,0:T(8,128)} fusion(bf16[256,12,128]{0,2,1:T(8,128)(2,1)S(1)} %bitcast.84, f32[12,256,896]{1,2,0:T(8,128)S(1)} %copy-done.3, f32[12,256]{1,0:T(8,128)S(1)} %get-tuple-element.64), kind=kOutput, calls=%fused_computation.34 | convolution fusion | flops 710148096 | bytes 17313792 | tf_op jit(solution)/shard_map/hqk,qhd->khd/dot_general | solution.py:84
  95.5 5.4 %fusion.4 = bf16[12,256,896]{1,2,0:T(8,128)(2,1)S(1)} fusion(f32[12,896,256]{2,1,0:T(8,128)} %get-tuple-element.67, f32[12,256]{1,0:T(8,128)S(1)} %get-tuple-element.66, f32[12,256,896]{1,2,0:T(8,128)S(1)} %copy-done.3, f32[12,256]{1,0:T(8,128)S(1)} %get-tuple-element.64), kind=kLoop, calls=%fused_computation.11 | loop fusion | flops 11010048 | bytes 27549696 | tf_op jit(solution)/shard_map/convert_element_type | solution.py:72
  101.0 4.1 %broadcast_multiply_fusion = f32[12,896,128]{1,2,0:T(8,128)} fusion(bf16[12,256,896]{1,2,0:T(8,128)(2,1)S(1)} %fusion.4, bf16[256,12,128]{0,2,1:T(8,128)(2,1)S(1)} %bitcast.80), kind=kOutput, calls=%fused_computation.33 | convolution fusion | flops 706019328 | bytes 11796480 | tf_op jit(solution)/shard_map/hqk,qhd->khd/dot_general | solution.py:79
  105.1 6.2 %copy.80 = f32[1,896,1536]{2,1,0:T(8,128)} copy(f32[1,896,1536]{1,2,0:T(8,128)} %bitcast.70) | data formatting | bytes 11010048 | tf_op jit(solution)/shard_map/stack;reshape | solution.py:86
  111.3 6.3 %copy.81 = f32[1,896,1536]{2,1,0:T(8,128)} copy(f32[1,896,1536]{1,2,0:T(8,128)} %bitcast.78) | data formatting | bytes 11010048 | tf_op jit(solution)/shard_map/stack;reshape | solution.py:86
  117.6 7.6 %fusion.1 = bf16[2,896,1536]{2,1,0:T(8,128)(2,1)} fusion(f32[1,896,1536]{2,1,0:T(8,128)} %copy.81, f32[1,896,1536]{2,1,0:T(8,128)} %copy.80), kind=kLoop, calls=%fused_computation.6 | loop fusion | flops 2752512 | bytes 16515072 | tf_op jit(solution)/shard_map/convert.7
  125.2 2.1 %fusion.32 = (bf16[2,64,1536]{2,1,0:T(8,128)(2,1)}, bf16[2,64,1536]{2,1,0:T(8,128)(2,1)}) fusion(bf16[2,896,1536]{2,1,0:T(8,128)(2,1)} %fusion.1), kind=kLoop, calls=%fused_computation.70 | loop fusion | bytes 1572864 | tf_op jit(solution)/shard_map/slice | solution.py:144
  127.2 3.4 %fusion.31 = (bf16[2,128,1536]{2,1,0:T(8,128)(2,1)S(1)}, bf16[2,128,1536]{2,1,0:T(8,128)(2,1)}, bf16[2,128,1536]{2,1,0:T(8,128)(2,1)}, bf16[2,128,1536]{2,1,0:T(8,128)(2,1)}) fusion(bf16[2,896,1536]{2,1,0:T(8,128)(2,1)} %fusion.1), kind=kLoop, calls=%fused_computation.69 | loop fusion | bytes 6291456 | tf_op jit(solution)/shard_map/slice | solution.py:148
  130.7 1.5 collective-permute-start.6
  133.3 2.3 %copy.82 = bf16[256,1536]{1,0:T(8,128)(2,1)} copy(bf16[256,1536]{0,1:T(8,128)(2,1)} %bitcast.85) | data formatting | bytes 1572864
  136.8 3.0 %collective-permute-start.7 = (bf16[2,64,1536]{2,1,0:T(8,128)(2,1)}, bf16[2,64,1536]{2,1,0:T(8,128)(2,1)S(1)}, u32[]{:S(2)}, u32[]{:S(2)}) collective-permute-start(bf16[2,64,1536]{2,1,0:T(8,128)(2,1)} %get-tuple-element.48), channel_id=1, source_target_pairs={{0,1},{1,2},{2,3},{3,4},{4,5},{5,6},{6,7},{7,8},{8,9},{9,10},{10,1... | collective-permute-start | bytes 1179656 | tf_op jit(solution)/shard_map/ppermute | solution.py:34
  139.9 6.7 %collective-permute-start.9 = (bf16[2,128,1536]{2,1,0:T(8,128)(2,1)}, bf16[2,128,1536]{2,1,0:T(8,128)(2,1)S(1)}, u32[]{:S(2)}, u32[]{:S(2)}) collective-permute-start(bf16[2,128,1536]{2,1,0:T(8,128)(2,1)} %get-tuple-element.46), channel_id=1, source_target_pairs={{0,2},{1,3},{2,0},{3,1},{4,6},{5,7},{6,4},{7,5},{8,10},{9,11},{10,... | collective-permute-start | bytes 2359304 | tf_op jit(solution)/shard_map/ppermute | solution.py:28
  146.6 2.8 %collective-permute-start.10 = (bf16[2,128,1536]{2,1,0:T(8,128)(2,1)}, bf16[2,128,1536]{2,1,0:T(8,128)(2,1)S(1)}, u32[]{:S(2)}, u32[]{:S(2)}) collective-permute-start(bf16[2,128,1536]{2,1,0:T(8,128)(2,1)} %get-tuple-element.45), channel_id=1, source_target_pairs={{0,4},{1,5},{2,6},{3,7},{4,0},{5,1},{6,2},{7,3},{8,12},{9,13},{10,... | collective-permute-start | bytes 2359304 | tf_op jit(solution)/shard_map/ppermute | solution.py:28
  149.4 2.1 %fusion.9 = f32[2,256,1536]{2,1,0:T(8,128)S(1)} fusion(f32[1,896,1536]{2,1,0:T(8,128)} %copy.80, f32[1,896,1536]{2,1,0:T(8,128)} %copy.81), kind=kLoop, calls=%fused_computation.19 | loop fusion | flops 786432 | bytes 14155776 | tf_op jit(solution)/shard_map/stack | solution.py:86
  152.2 12.3 %collective-permute-done.9 = bf16[2,128,1536]{2,1,0:T(8,128)(2,1)S(1)} collective-permute-done((bf16[2,128,1536]{2,1,0:T(8,128)(2,1)}, bf16[2,128,1536]{2,1,0:T(8,128)(2,1)S(1)}, u32[]{:S(2)}, u32[]{:S(2)}) %collective-permute-start.9) | collective-permute-done | bytes 786464 | tf_op jit(solution)/shard_map/ppermute | solution.py:28
  164.8 15.6 %collective-permute-done.10 = bf16[2,128,1536]{2,1,0:T(8,128)(2,1)S(1)} collective-permute-done((bf16[2,128,1536]{2,1,0:T(8,128)(2,1)}, bf16[2,128,1536]{2,1,0:T(8,128)(2,1)S(1)}, u32[]{:S(2)}, u32[]{:S(2)}) %collective-permute-start.10) | collective-permute-done | bytes 786464 | tf_op jit(solution)/shard_map/ppermute | solution.py:28
  180.7 7.9 %collective-permute-done.11 = bf16[2,128,1536]{2,1,0:T(8,128)(2,1)S(1)} collective-permute-done((bf16[2,128,1536]{2,1,0:T(8,128)(2,1)S(1)}, bf16[2,128,1536]{2,1,0:T(8,128)(2,1)S(1)}, u32[]{:S(2)}, u32[]{:S(2)}) %collective-permute-start.11) | collective-permute-done | bytes 786464 | tf_op jit(solution)/shard_map/ppermute | solution.py:28
  (74 shorter events, 19.6 us)
Async XLA Ops:
  2.0 5.3 %copy-start.8 = (s32[1,4]{1,0:T(1,128)S(1)}, s32[1,4]{1,0:T(1,128)}, u32[]{:S(2)}) copy-start(s32[1,4]{1,0:T(1,128)} %param.15) | copy-start | bytes 52
  3.8 15.5 %copy-start.9 = (s32[1,4,2]{1,2,0:T(2,128)S(1)}, s32[1,4,2]{1,2,0:T(2,128)}, u32[]{:S(2)}) copy-start(s32[1,4,2]{1,2,0:T(2,128)} %param.14) | copy-start | bytes 100
  4.8 15.7 %copy-start.6 = (bf16[256,1536]{1,0:T(8,128)(2,1)S(1)}, bf16[256,1536]{1,0:T(8,128)(2,1)}, u32[]{:S(2)}) copy-start(bf16[256,1536]{1,0:T(8,128)(2,1)} %param.10) | copy-start | bytes 2359300
  4.8 19.2 %collective-permute-start = (bf16[2,64,1536]{2,1,0:T(8,128)(2,1)}, bf16[2,64,1536]{2,1,0:T(8,128)(2,1)S(1)}, u32[]{:S(2)}, u32[]{:S(2)}) collective-permute-start(bf16[2,64,1536]{2,1,0:T(8,128)(2,1)} %copy.66), channel_id=1, source_target_pairs={{0,1},{1,2},{2,3},{3,4},{4,5},{5,6},{6,7},{7,8},{8,9},{9,10},{10,1... | collective-permute-start | bytes 1179656 | tf_op jit(solution)/shard_map/ppermute | solution.py:17
  12.5 16.8 %collective-permute-start.2 = (bf16[2,128,1536]{1,2,0:T(8,128)(2,1)}, bf16[2,128,1536]{1,2,0:T(8,128)(2,1)}, u32[]{:S(2)}, u32[]{:S(2)}) collective-permute-start(bf16[2,128,1536]{1,2,0:T(8,128)(2,1)} %get-tuple-element.55), channel_id=1, source_target_pairs={{0,1},{1,0},{2,3},{3,2},{4,5},{5,4},{6,7},{7,6},{8,9},{9,8},{10,11... | collective-permute-start | bytes 2359304 | tf_op jit(solution)/shard_map/ppermute | solution.py:28
  15.1 19.8 %collective-permute-start.3 = (bf16[2,128,1536]{1,2,0:T(8,128)(2,1)}, bf16[2,128,1536]{1,2,0:T(8,128)(2,1)}, u32[]{:S(2)}, u32[]{:S(2)}) collective-permute-start(bf16[2,128,1536]{1,2,0:T(8,128)(2,1)} %get-tuple-element.56), channel_id=1, source_target_pairs={{0,2},{1,3},{2,0},{3,1},{4,6},{5,7},{6,4},{7,5},{8,10},{9,11},{10,... | collective-permute-start | bytes 2359304 | tf_op jit(solution)/shard_map/ppermute | solution.py:28
  16.6 36.2 %collective-permute-start.4 = (bf16[2,128,1536]{1,2,0:T(8,128)(2,1)}, bf16[2,128,1536]{1,2,0:T(8,128)(2,1)}, u32[]{:S(2)}, u32[]{:S(2)}) collective-permute-start(bf16[2,128,1536]{1,2,0:T(8,128)(2,1)} %get-tuple-element.57), channel_id=1, source_target_pairs={{0,4},{1,5},{2,6},{3,7},{4,0},{5,1},{6,2},{7,3},{8,12},{9,13},{10,... | collective-permute-start | bytes 2359304 | tf_op jit(solution)/shard_map/ppermute | solution.py:28
  18.2 37.1 %collective-permute-start.5 = (bf16[2,128,1536]{1,2,0:T(8,128)(2,1)}, bf16[2,128,1536]{1,2,0:T(8,128)(2,1)}, u32[]{:S(2)}, u32[]{:S(2)}) collective-permute-start(bf16[2,128,1536]{1,2,0:T(8,128)(2,1)} %get-tuple-element.54), channel_id=1, source_target_pairs={{0,8},{1,9},{2,10},{3,11},{4,12},{5,13},{6,14},{7,15},{8,0},{9,1},... | collective-permute-start | bytes 2359304 | tf_op jit(solution)/shard_map/ppermute | solution.py:28
  24.0 4.0 %collective-permute-start.1 = (bf16[2,64,1536]{2,1,0:T(8,128)(2,1)}, bf16[2,64,1536]{2,1,0:T(8,128)(2,1)}, u32[]{:S(2)}, u32[]{:S(2)}) collective-permute-start(bf16[2,64,1536]{2,1,0:T(8,128)(2,1)} %copy.67), channel_id=1, source_target_pairs={{1,0},{2,1},{3,2},{4,3},{5,4},{6,5},{7,6},{8,7},{9,8},{10,9},{11,1... | collective-permute-start | bytes 1179656 | tf_op jit(solution)/shard_map/ppermute | solution.py:20
  64.5 4.7 %copy-start.4 = (bf16[256,1536]{0,1:T(8,128)(2,1)S(1)}, bf16[256,1536]{0,1:T(8,128)(2,1)}, u32[]{:S(2)}) copy-start(bf16[256,1536]{0,1:T(8,128)(2,1)} %copy.70) | copy-start | bytes 2359300
  69.2 7.6 %copy-start.1 = (bf16[1,896,1536]{1,2,0:T(8,128)(2,1)}, bf16[1,896,1536]{1,2,0:T(8,128)(2,1)S(1)}, u32[]{:S(2)}) copy-start(bf16[1,896,1536]{1,2,0:T(8,128)(2,1)S(1)} %get-tuple-element.50) | copy-start | bytes 8257540
  76.9 8.4 %copy-start.3 = (f32[12,256,896]{1,2,0:T(8,128)S(1)}, f32[12,256,896]{1,2,0:T(8,128)}, u32[]{:S(2)}) copy-start(f32[12,256,896]{1,2,0:T(8,128)} %get-tuple-element.65) | copy-start | bytes 33030148
  76.9 9.2 %copy-start.5 = (bf16[1,896,1536]{1,2,0:T(8,128)(2,1)S(1)}, bf16[1,896,1536]{1,2,0:T(8,128)(2,1)}, u32[]{:S(2)}) copy-start(bf16[1,896,1536]{1,2,0:T(8,128)(2,1)} %get-tuple-element.51) | copy-start | bytes 8257540
  76.9 9.3 %copy-start.7 = (bf16[256,1536]{0,1:T(8,128)(2,1)S(1)}, bf16[256,1536]{0,1:T(8,128)(2,1)}, u32[]{:S(2)}) copy-start(bf16[256,1536]{0,1:T(8,128)(2,1)} %copy.74) | copy-start | bytes 2359300
  101.0 4.1 %copy-start = (bf16[12,256,896]{1,2,0:T(8,128)(2,1)}, bf16[12,256,896]{1,2,0:T(8,128)(2,1)S(1)}, u32[]{:S(2)}) copy-start(bf16[12,256,896]{1,2,0:T(8,128)(2,1)S(1)} %fusion.4) | copy-start | bytes 16515076
  111.3 20.9 %slice-start.4 = ((s8[5505024]{0:T(1024)(128)(4,1)}), s8[1310720]{0:T(1024)(128)(4,1)S(1)}, s32[]{:S(2)}) async-start(s8[5505024]{0:T(1024)(128)(4,1)} %bitcast.66), calls=%async_computation.4 | async-start | bytes 2621440
  117.6 14.6 %slice-start.5 = ((s8[5505024]{0:T(1024)(128)(4,1)}), s8[4194304]{0:T(1024)(128)(4,1)S(1)}, s32[]{:S(2)}) async-start(s8[5505024]{0:T(1024)(128)(4,1)} %bitcast.66), calls=%async_computation.5 | async-start | bytes 8388608
  127.2 5.0 %copy-start.2 = (bf16[1,896,1536]{1,2,0:T(8,128)(2,1)S(1)}, bf16[1,896,1536]{1,2,0:T(8,128)(2,1)}, u32[]{:S(2)}) copy-start(bf16[1,896,1536]{1,2,0:T(8,128)(2,1)} %copy-done.1) | copy-start | bytes 8257540
  130.7 20.8 %collective-permute-start.6 = (bf16[2,64,1536]{2,1,0:T(8,128)(2,1)}, bf16[2,64,1536]{2,1,0:T(8,128)(2,1)S(1)}, u32[]{:S(2)}, u32[]{:S(2)}) collective-permute-start(bf16[2,64,1536]{2,1,0:T(8,128)(2,1)} %get-tuple-element.49), channel_id=1, source_target_pairs={{1,0},{2,1},{3,2},{4,3},{5,4},{6,5},{7,6},{8,7},{9,8},{10,9},{11,1... | collective-permute-start | bytes 1179656 | tf_op jit(solution)/shard_map/ppermute | solution.py:34
  135.6 16.0 %slice-start.2 = ((s8[5505024]{0:T(1024)(128)(4,1)}), s8[1310720]{0:T(1024)(128)(4,1)S(1)}, s32[]{:S(2)}) async-start(s8[5505024]{0:T(1024)(128)(4,1)} %bitcast.64), calls=%async_computation.2 | async-start | bytes 2621440
  136.8 15.0 %collective-permute-start.7 = (bf16[2,64,1536]{2,1,0:T(8,128)(2,1)}, bf16[2,64,1536]{2,1,0:T(8,128)(2,1)S(1)}, u32[]{:S(2)}, u32[]{:S(2)}) collective-permute-start(bf16[2,64,1536]{2,1,0:T(8,128)(2,1)} %get-tuple-element.48), channel_id=1, source_target_pairs={{0,1},{1,2},{2,3},{3,4},{4,5},{5,6},{6,7},{7,8},{8,9},{9,10},{10,1... | collective-permute-start | bytes 1179656 | tf_op jit(solution)/shard_map/ppermute | solution.py:34
  139.8 12.1 %collective-permute-start.8 = (bf16[2,128,1536]{2,1,0:T(8,128)(2,1)}, bf16[2,128,1536]{2,1,0:T(8,128)(2,1)S(1)}, u32[]{:S(2)}, u32[]{:S(2)}) collective-permute-start(bf16[2,128,1536]{2,1,0:T(8,128)(2,1)} %get-tuple-element.47), channel_id=1, source_target_pairs={{0,1},{1,0},{2,3},{3,2},{4,5},{5,4},{6,7},{7,6},{8,9},{9,8},{10,11... | collective-permute-start | bytes 2359304 | tf_op jit(solution)/shard_map/ppermute | solution.py:28
  139.9 24.7 %collective-permute-start.9 = (bf16[2,128,1536]{2,1,0:T(8,128)(2,1)}, bf16[2,128,1536]{2,1,0:T(8,128)(2,1)S(1)}, u32[]{:S(2)}, u32[]{:S(2)}) collective-permute-start(bf16[2,128,1536]{2,1,0:T(8,128)(2,1)} %get-tuple-element.46), channel_id=1, source_target_pairs={{0,2},{1,3},{2,0},{3,1},{4,6},{5,7},{6,4},{7,5},{8,10},{9,11},{10,... | collective-permute-start | bytes 2359304 | tf_op jit(solution)/shard_map/ppermute | solution.py:28
  146.6 5.0 %slice-start = ((s8[5505024]{0:T(1024)(128)(4,1)}), s8[4194304]{0:T(1024)(128)(4,1)S(1)}, s32[]{:S(2)}) async-start(s8[5505024]{0:T(1024)(128)(4,1)} %bitcast.62), calls=%async_computation | async-start | bytes 8388608
  146.6 5.0 %slice-start.1 = ((s8[5505024]{0:T(1024)(128)(4,1)}), s8[1310720]{0:T(1024)(128)(4,1)S(1)}, s32[]{:S(2)}) async-start(s8[5505024]{0:T(1024)(128)(4,1)} %bitcast.62), calls=%async_computation.1 | async-start | bytes 2621440
  146.6 5.1 %slice-start.3 = ((s8[5505024]{0:T(1024)(128)(4,1)}), s8[4194304]{0:T(1024)(128)(4,1)S(1)}, s32[]{:S(2)}) async-start(s8[5505024]{0:T(1024)(128)(4,1)} %bitcast.64), calls=%async_computation.3 | async-start | bytes 8388608
  146.6 33.8 %collective-permute-start.10 = (bf16[2,128,1536]{2,1,0:T(8,128)(2,1)}, bf16[2,128,1536]{2,1,0:T(8,128)(2,1)S(1)}, u32[]{:S(2)}, u32[]{:S(2)}) collective-permute-start(bf16[2,128,1536]{2,1,0:T(8,128)(2,1)} %get-tuple-element.45), channel_id=1, source_target_pairs={{0,4},{1,5},{2,6},{3,7},{4,0},{5,1},{6,2},{7,3},{8,12},{9,13},{10,... | collective-permute-start | bytes 2359304 | tf_op jit(solution)/shard_map/ppermute | solution.py:28
  151.5 37.1 %collective-permute-start.11 = (bf16[2,128,1536]{2,1,0:T(8,128)(2,1)S(1)}, bf16[2,128,1536]{2,1,0:T(8,128)(2,1)S(1)}, u32[]{:S(2)}, u32[]{:S(2)}) collective-permute-start(bf16[2,128,1536]{2,1,0:T(8,128)(2,1)S(1)} %get-tuple-element.44), channel_id=1, source_target_pairs={{0,8},{1,9},{2,10},{3,11},{4,12},{5,13},{6,14},{7,15},{8,0},{9,1},... | collective-permute-start | bytes 2359304 | tf_op jit(solution)/shard_map/ppermute | solution.py:28
where the time goes:
time: 192 us; the launch traced here: 190 us
  waiting for transfers between devices  62.8 us (33%)
  local copies, waits for them, and re-layouts  49.8 us (26%)
  matrix products  29.1 us (15%)
  starting transfers between devices  24.9 us (13%)
  other arithmetic  20.2 us (11%)
  between operations  3.57 us (2%)
    ppermute x8, waiting for transfers between devices, partner(): return lax.ppermute(value, axis, pairs)  61.8 us
    ppermute x8, starting transfers between devices, partner(): return lax.ppermute(value, axis, pairs)  16.4 us
    another operation x2, local copies, waits for them, and re-layouts, backward_part(): jnp.stack([key_term.reshape(count, -1), value_term.reshape(count, -1)])  12.5 us
    unnamed x38, local copies, waits for them, and re-layouts  12.1 us
    concatenate x1, local copies, waits for them, and re-layouts, fetch_keys(): return jnp.concatenate(pieces, axis=1)  9.2 us
    another operation x2, other arithmetic  7.76 us
    sub x1, matrix products, forward_part(): weights = jnp.exp(scores - highest)  7.61 us
    dot_general x1, matrix products, forward_part(): jnp.einsum('hqk,khd->qhd', rounded, split_heads(value_blk), preferred_ele...  6.99 us
  transfers between devices with their start and end apart: 12, of which 7 were waited for; matrix products, arithmetic and copies ran while one was open for 9% of the time, Pallas kernels for 0%

commit v1 on v0

v1 whole, which is shorter than its diff:
```python
import functools

import jax
import jax.numpy as jnp
from jax import lax
from jax.experimental import pallas as pl
from jax.experimental.pallas import tpu as pltpu
from jax.sharding import PartitionSpec as P

HDIM = 128
BLK = 128
EDGE = 64
SCALE = HDIM ** (-0.5)
LOG2E = 1.4426950408889634
MASKED = -1e30
SPLIT = (6, 6)

F32 = jnp.float32
BF16 = jnp.bfloat16
ANY = pl.BlockSpec(memory_space=pl.ANY)
NT = (((1,), (1,)), ((), ()))
TN = (((0,), (0,)), ((), ()))


def dot(lhs, rhs, dims=(((1,), (0,)), ((), ()))):
    return lax.dot_general(lhs, rhs, dims, preferred_element_type=F32)


def cost(flops, moved, exps=0):
    return pl.CostEstimate(flops=flops, bytes_accessed=moved, transcendentals=exps)


def pack_kernel(rows, col, where_ref, k_ref, v_ref, *rest):
    outs, sem = rest[:-1], rest[-1]
    width = outs[0].shape[2]
    copies = []
    for out, parts in zip(outs, rows, strict=True):
        at = 0
        for index, size in parts:
            start = pl.multiple_of(where_ref[index], EDGE)
            for side, src in enumerate((k_ref, v_ref)):
                copies.append(
                    pltpu.make_async_copy(
                        src.at[pl.ds(start, size), pl.ds(col, width)],
                        out.at[side, pl.ds(at, size)],
                        sem.at[len(copies)],
                    )
                )
            at += size
    for copy in copies:
        copy.start()
    for copy in copies:
        copy.wait()


def pack(where, keys, values, rows, col, width):
    shapes = [
        jax.ShapeDtypeStruct((2, sum(size for _, size in parts), width), BF16) for parts in rows
    ]
    count = 2 * sum(len(parts) for parts in rows)
    return pl.pallas_call(
        functools.partial(pack_kernel, rows, col),
        out_shape=shapes,
        in_specs=[pl.BlockSpec(memory_space=pltpu.SMEM), ANY, ANY],
        out_specs=[ANY] * len(shapes),
        scratch_shapes=[pltpu.SemaphoreType.DMA((count,))],
        compiler_params=pltpu.CompilerParams(vmem_limit_bytes=1 << 20),
        cost_estimate=cost(0, sum(4 * s.size for s in shapes)),
    )(where, keys, values)


def attend_kernel(first, parts, *refs):
    count = len(parts)
    q_ref, g_ref, k_ref, v_ref, bias_ref = refs[:5]
    got = refs[5 : 5 + count]
    refs = refs[5 + count + (0 if first else 2) :]
    o_ref, dq_ref, own_ref = refs[:3]
    back = refs[3 : 3 + count]
    keys, vals = refs[3 + count :]
    tokens = q_ref.shape[0]
    keys[0:tokens] = k_ref[...]
    vals[0:tokens] = v_ref[...]
    at = tokens
    for ref, size in zip(got, parts, strict=True):
        keys[at : at + size] = ref[0]
        vals[at : at + size] = ref[1]
        at += size
    query, grad, key, val = q_ref[...], g_ref[...], keys[...], vals[...]
    blocks = tokens // BLK
    bias = jnp.concatenate(
        [jnp.broadcast_to(bias_ref[b : b + 1], (BLK, at)) for b in range(blocks)], axis=0
    )
    scores = dot(query, key, NT) * (SCALE * LOG2E) + bias
    weights = jnp.exp2(scores - jnp.max(scores, axis=1, keepdims=True))
    weights = weights * (1.0 / jnp.sum(weights, axis=1, keepdims=True))
    rounded = weights.astype(BF16)
    o_ref[...] = dot(rounded, val).astype(BF16)
    dprob = dot(grad, val, NT)
    inner = jnp.sum(weights * dprob, axis=1, keepdims=True)
    dscore = (weights * (dprob - inner)).astype(BF16)
    dq_ref[...] = (dot(dscore, key) * SCALE).astype(BF16)
    terms = (dot(dscore, query, TN) * SCALE, dot(rounded, grad, TN))
    for side, term in enumerate(terms):
        own_ref[side] = term[:tokens]
        at = tokens
        for ref, size in zip(back, parts, strict=True):
            ref[side] = term[at : at + size].astype(BF16)
            at += size


def attend(queries, out_grad, keys, values, bias, got, previous, head, heads):
    tokens, feat = queries.shape
    width = heads * HDIM
    parts = [piece.shape[1] for piece in got]
    total = tokens + sum(parts)
    column = pl.BlockSpec((tokens, HDIM), lambda h: (0, head + h))
    piece_specs = [pl.BlockSpec((2, size, HDIM), lambda h: (0, 0, h)) for size in parts]
    out_shape = [
        jax.ShapeDtypeStruct((tokens, feat), BF16),
        jax.ShapeDtypeStruct((tokens, feat), BF16),
        jax.ShapeDtypeStruct((2, tokens, width), F32),
    ] + [jax.ShapeDtypeStruct((2, size, width), BF16) for size in parts]
    inputs = [queries, out_grad, keys, values, bias, *got]
    specs = [column] * 4 + [pl.BlockSpec(bias.shape, lambda h: (0, 0))] + piece_specs
    aliases = {}
    if previous is not None:
        aliases = {len(inputs): 0, len(inputs) + 1: 1}
        inputs += list(previous)
        specs += [ANY, ANY]
    return pl.pallas_call(
        functools.partial(attend_kernel, previous is None, parts),
        out_shape=out_shape,
        grid=(heads,),
        in_specs=specs,
        out_specs=[column, column, pl.BlockSpec((2, tokens, HDIM), lambda h: (0, 0, h))]
        + piece_specs,
        scratch_shapes=[pltpu.VMEM((total, HDIM), BF16)] * 2,
        input_output_aliases=aliases,
        compiler_params=pltpu.CompilerParams(
            dimension_semantics=("arbitrary",), vmem_limit_bytes=40 << 20
        ),
        cost_estimate=cost(
            12 * tokens * total * width,
            2 * width * (6 * tokens + 4 * tokens + 4 * (total - tokens)),
            tokens * total * heads,
        ),
    )(*inputs)


def combine_kernel(first, rows, where_ref, own_ref, *refs):
    got = refs[: len(rows)]
    refs = refs[len(rows) + (0 if first else 2) :]
    outs, acc = refs[:2], refs[2]
    acc[...] = own_ref[...]
    for ref, parts in zip(got, rows, strict=True):
        at = 0
        for index, size in parts:
            spot = pl.ds(pl.multiple_of(where_ref[index], EDGE), size)
            for side in range(2):
                acc[side, spot] += ref[side, at : at + size].astype(F32)
            at += size
    for side in range(2):
        outs[side][...] = acc[side].astype(BF16)


def combine(where, own, got, rows, previous, head, heads, feat):
    tokens = own.shape[1]
    inputs = [where, own, *got]
    specs = [
        pl.BlockSpec(memory_space=pltpu.SMEM),
        pl.BlockSpec((2, tokens, HDIM), lambda h: (0, 0, h)),
    ] + [pl.BlockSpec((2, piece.shape[1], HDIM), lambda h: (0, 0, h)) for piece in got]
    aliases = {}
    if previous is not None:
        aliases = {len(inputs): 0, len(inputs) + 1: 1}
        inputs += list(previous)
        specs += [ANY, ANY]
    column = pl.BlockSpec((tokens, HDIM), lambda h: (0, head + h))
    return pl.pallas_call(
        functools.partial(combine_kernel, previous is None, rows),
        out_shape=[jax.ShapeDtypeStruct((tokens, feat), BF16)] * 2,
        grid=(heads,),
        in_specs=specs,
        out_specs=[column, column],
        scratch_shapes=[pltpu.VMEM((2, tokens, HDIM), F32)],
        input_output_aliases=aliases,
        compiler_params=pltpu.CompilerParams(
            dimension_semantics=("arbitrary",), vmem_limit_bytes=16 << 20
        ),
        cost_estimate=cost(
            0, sum(2 * piece.size for piece in got) + 6 * own.size
        ),
    )(*inputs)


def per_device(queries, key_rows, value_rows, out_grad, block_mask, block_pick):
    frames = lax.axis_size("frame")
    levels = frames.bit_length() - 1
    device = lax.axis_index("frame")
    tokens, feat = queries.shape
    blocks = tokens // BLK
    odd = device % 2
    where = jnp.concatenate(
        [
            block_pick[0] * BLK,
            jnp.stack([(1 - odd) * (tokens - EDGE), odd * (tokens - EDGE)]).astype(jnp.int32),
        ]
    )
    rows = [[(level, BLK)] for level in range(levels - 1, 0, -1)]
    rows += [[(0, BLK), (levels, EDGE)], [(levels + 1, EDGE)]]
    pairs = [[(f, f ^ (1 << level)) for f in range(frames)] for level in range(levels - 1, -1, -1)]
    beyond = [f + (1 if f % 2 else -1) for f in range(frames)]
    pairs.append([(f, g if 0 <= g < frames else f) for f, g in enumerate(beyond)])

    def bias_of(seen, size):
        return jnp.broadcast_to(jnp.where(seen, 0.0, MASKED).astype(F32)[:, None], (blocks, size))

    mask = block_mask[0] > 0
    always = jnp.ones((blocks,), bool)
    beside = (device > 0) & (device < frames - 1)
    bias = [bias_of(always, tokens)]
    bias += [bias_of(mask[level], BLK) for level in range(levels - 1, -1, -1)]
    bias += [bias_of(always, EDGE), bias_of(always & beside, EDGE)]
    bias = jnp.concatenate(bias, axis=1)

    head = 0
    sent = []
    for heads in SPLIT:
        pieces = pack(where, key_rows, value_rows, rows, head * HDIM, heads * HDIM)
        sent.append([lax.ppermute(p, "frame", to) for p, to in zip(pieces, pairs, strict=True)])
        head += heads
    head = 0
    outs = None
    returned = []
    for heads, got in zip(SPLIT, sent, strict=True):
        attended, query_grad, own, *terms = attend(
            queries, out_grad, key_rows, value_rows, bias, got, outs, head, heads
        )
        outs = (attended, query_grad)
        returned.append(
            (own, [lax.ppermute(t, "frame", to) for t, to in zip(terms, pairs, strict=True)])
        )
        head += heads
    head = 0
    grads = None
    for heads, (own, got) in zip(SPLIT, returned, strict=True):
        grads = combine(where, own, got, rows, grads, head, heads, feat)
        head += heads
    return (*outs, *grads)


def solution(mesh):
    flat = P(("group", "frame"), None)
    return jax.shard_map(
        per_device,
        mesh=mesh,
        in_specs=(flat, flat, flat, flat, P(("group", "frame"), None, None), flat),
        out_specs=(flat, flat, flat, flat),
        check_vma=False,
    )
```

time: 192 us -> 107 us (0.56)
  waiting for transfers between devices: 62.8 us -> 23.4 us
  local copies, waits for them, and re-layouts: 49.8 us -> 14.2 us
  Pallas kernels: 0 us -> 32.2 us
  matrix products: 29.1 us -> 0 us
  other arithmetic: 20.2 us -> 0.96 us
  starting transfers between devices: 24.9 us -> 33.8 us
  between operations: 3.57 us -> 0.79 us
    ppermute x12 -> x20, waiting for transfers between devices: 62.8 us -> 23.4 us  [the longest x10 20.5 us: per_device(): lax.ppermute(t, 'frame', to)]
    pallas_call x0 -> x6, Pallas kernels: none -> 32.2 us  [the longest x2 22.4 us: attend(): pl.pallas_call(functools.partial(attend_kernel, previous is None, parts),...]
    dot_general x5 -> x0, matrix products: 21.5 us -> none  [the longest x1 6.99 us: forward_part(): jnp.einsum('hqk,khd->qhd', rounded, split_heads(value_blk), preferred_ele...]
    slice x6 -> x0, local copies, waits for them, and re-layouts: 12.9 us -> none  [the longest x1 4.74 us: per_device(): gathered[0]]
    another operation x2 -> x0, local copies, waits for them, and re-layouts: 12.5 us -> none  [backward_part(): jnp.stack([key_term.reshape(count, -1), value_term.reshape(count, -1)])]
    another operation x6 -> x0, other arithmetic: 12.3 us -> none
    ppermute x12 -> x20, starting transfers between devices: 24.9 us -> 33.8 us  [the longest x10 24.2 us: per_device(): lax.ppermute(p, 'frame', to)]
    concatenate x1, local copies, waits for them, and re-layouts: 9.2 us -> 0.78 us  [per_device(): bias = jnp.concatenate(bias, axis=1)]
  transfers between devices with their start and end apart: 12 -> 20, of which waited for: 7 -> 4; matrix products, arithmetic and copies ran while one was open for 9% -> 4% of each run, Pallas kernels for 0% -> 26%
where the time goes in v1:
time: 107 us; the launch traced here: 105 us
  starting transfers between devices  33.8 us (32%)
  Pallas kernels  32.2 us (30%)
  waiting for transfers between devices  23.4 us (22%)
  local copies, waits for them, and re-layouts  14.2 us (13%)
    ppermute x10, starting transfers between devices, per_device(): lax.ppermute(p, 'frame', to)  24.2 us
    pallas_call x2, Pallas kernels, attend(): pl.pallas_call(functools.partial(attend_kernel, previous is None, parts),...  22.4 us
    ppermute x10, waiting for transfers between devices, per_device(): lax.ppermute(t, 'frame', to)  20.5 us
    unnamed x32, local copies, waits for them, and re-layouts  9.76 us
    ppermute x10, starting transfers between devices, per_device(): lax.ppermute(t, 'frame', to)  9.56 us
    pallas_call x2, Pallas kernels, combine(): pl.pallas_call(functools.partial(combine_kernel, previous is None, rows),...  6.39 us
    broadcast_in_dim x7, local copies, waits for them, and re-layouts, bias_of(): jnp.broadcast_to(jnp.where(seen, 0.0, MASKED).astype(F32)[:, None], (bloc...  3.7 us
    pallas_call x2, Pallas kernels, pack(): pl.pallas_call(functools.partial(pack_kernel, rows, col), out_shape=shape...  3.41 us
  transfers between devices with their start and end apart: 20, of which 4 were waited for; matrix products, arithmetic and copies ran while one was open for 4% of the time, Pallas kernels for 26%

profile of v1, /device:TPU:0, one launch (start us, length us, event | category | flops | bytes accessed | tf_op | source)
XLA Modules:
  0.0 105.4 jit_solution(1398682013115640530)
XLA Ops:
  1.4 1.1 %copy-done = bf16[256,1536]{1,0:T(8,128)(2,1)S(1)} copy-done((bf16[256,1536]{1,0:T(8,128)(2,1)S(1)}, bf16[256,1536]{1,0:T(8,128)(2,1)}, u32[]{:S(2)}) %copy-start) | copy-done | bytes 786456
  2.5 1.1 %copy-done.2 = bf16[256,1536]{1,0:T(8,128)(2,1)S(1)} copy-done((bf16[256,1536]{1,0:T(8,128)(2,1)S(1)}, bf16[256,1536]{1,0:T(8,128)(2,1)}, u32[]{:S(2)}) %copy-start.2) | copy-done | bytes 786456
  3.7 1.6 %shard_map.94 = (bf16[2,128,768]{2,1,0:T(8,128)(2,1)S(1)}, bf16[2,128,768]{2,1,0:T(8,128)(2,1)S(1)}, bf16[2,128,768]{2,1,0:T(8,128)(2,1)S(1)}, bf16[2,192,768]{2,1,0:T(8,128)(2,1)}, bf16[2,64,768]{2,1,0:T(8,128)(2,1)S(1)}) custom-call(s32[6]{0:T(128)S(1)} %pad_add_fusion.where_ref, bf16[256,1536]{1,0:T(8,128)(2,1)S(1)} %copy-done, ...), custom_call_target="tpu_custom_call" | custom-call | bytes 3932160 | tf_op jit(solution)/shard_map/pallas_call | solution.py:61
  5.2 4.1 %collective-permute-start.5 = (bf16[2,128,768]{2,1,0:T(8,128)(2,1)S(1)}, bf16[2,128,768]{2,1,0:T(8,128)(2,1)S(1)}, u32[]{:S(2)}, u32[]{:S(2)}) collective-permute-start(bf16[2,128,768]{2,1,0:T(8,128)(2,1)S(1)} %get-tuple-element.39), channel_id=1, source_target_pairs={{0,8},{1,9},{2,10},{3,11},{4,12},{5,13},{6,14},{7,15},{8,0},{9,1},... | collective-permute-start | bytes 1179656 | tf_op jit(solution)/shard_map/ppermute | solution.py:230
  9.3 1.6 %collective-permute-start.6 = (bf16[2,128,768]{2,1,0:T(8,128)(2,1)S(1)}, bf16[2,128,768]{2,1,0:T(8,128)(2,1)S(1)}, u32[]{:S(2)}, u32[]{:S(2)}) collective-permute-start(bf16[2,128,768]{2,1,0:T(8,128)(2,1)S(1)} %get-tuple-element.40), channel_id=1, source_target_pairs={{0,4},{1,5},{2,6},{3,7},{4,0},{5,1},{6,2},{7,3},{8,12},{9,13},{10,... | collective-permute-start | bytes 1179656 | tf_op jit(solution)/shard_map/ppermute | solution.py:230
  10.9 1.5 %collective-permute-start.7 = (bf16[2,128,768]{2,1,0:T(8,128)(2,1)S(1)}, bf16[2,128,768]{2,1,0:T(8,128)(2,1)S(1)}, u32[]{:S(2)}, u32[]{:S(2)}) collective-permute-start(bf16[2,128,768]{2,1,0:T(8,128)(2,1)S(1)} %get-tuple-element.41), channel_id=1, source_target_pairs={{0,2},{1,3},{2,0},{3,1},{4,6},{5,7},{6,4},{7,5},{8,10},{9,11},{10,... | collective-permute-start | bytes 1179656 | tf_op jit(solution)/shard_map/ppermute | solution.py:230
  13.1 1.8 %shard_map.93 = (bf16[2,128,768]{2,1,0:T(8,128)(2,1)}, bf16[2,128,768]{2,1,0:T(8,128)(2,1)}, bf16[2,128,768]{2,1,0:T(8,128)(2,1)}, bf16[2,192,768]{2,1,0:T(8,128)(2,1)}, bf16[2,64,768]{2,1,0:T(8,128)(2,1)S(1)}) custom-call(s32[6]{0:T(128)S(1)} %pad_add_fusion.where_ref, bf16[256,1536]{1,0:T(8,128)(2,1)S(1)} %copy-done.1, bf16[256,1536]{1,0:T(8,128)(2,1)S(1)} %copy-done.3), custom_call_target="tpu_custom_call" | custom-call | bytes 3932160 | tf_op jit(solution)/shard_map/pallas_call | solution.py:61
  15.0 0.7 copy-done.14
  15.6 0.7 copy-done.12
  16.3 7.8 %collective-permute-start.3 = (bf16[2,192,768]{2,1,0:T(8,128)(2,1)}, bf16[2,192,768]{2,1,0:T(8,128)(2,1)}, u32[]{:S(2)}, u32[]{:S(2)}) collective-permute-start(bf16[2,192,768]{2,1,0:T(8,128)(2,1)} %get-tuple-element.37), channel_id=1, source_target_pairs={{0,1},{1,0},{2,3},{3,2},{4,5},{5,4},{6,7},{7,6},{8,9},{9,8},{10,11... | collective-permute-start | bytes 1769480 | tf_op jit(solution)/shard_map/ppermute | solution.py:230
  24.1 2.9 %collective-permute-done.5.refs_5_ = bf16[2,128,768]{2,1,0:T(8,128)(2,1)S(1)} collective-permute-done((bf16[2,128,768]{2,1,0:T(8,128)(2,1)S(1)}, bf16[2,128,768]{2,1,0:T(8,128)(2,1)S(1)}, u32[]{:S(2)}, u32[]{:S(2)}) %collective-permute-start.5) | collective-permute-done | bytes 393248 | tf_op jit(solution)/shard_map/ppermute | solution.py:230
  27.0 0.7 copy-done.6
  27.7 6.3 %collective-permute-start = (bf16[2,128,768]{2,1,0:T(8,128)(2,1)}, bf16[2,128,768]{2,1,0:T(8,128)(2,1)S(1)}, u32[]{:S(2)}, u32[]{:S(2)}) collective-permute-start(bf16[2,128,768]{2,1,0:T(8,128)(2,1)} %get-tuple-element.34), channel_id=1, source_target_pairs={{0,8},{1,9},{2,10},{3,11},{4,12},{5,13},{6,14},{7,15},{8,0},{9,1},... | collective-permute-start | bytes 1179656 | tf_op jit(solution)/shard_map/ppermute | solution.py:230
  34.0 0.7 copy-done.8
  34.8 0.7 collective-permute-start.1
  35.5 0.7 copy-done.10
  40.2 0.8 concatenate.6.refs_4_
  41.0 1.6 %collective-permute-start.4 = (bf16[2,64,768]{2,1,0:T(8,128)(2,1)}, bf16[2,64,768]{2,1,0:T(8,128)(2,1)S(1)}, u32[]{:S(2)}, u32[]{:S(2)}) collective-permute-start(bf16[2,64,768]{2,1,0:T(8,128)(2,1)} %copy-done.14), channel_id=1, source_target_pairs={{0,0},{1,2},{2,1},{3,4},{4,3},{5,6},{6,5},{7,8},{8,7},{9,10},{10,9... | collective-permute-start | bytes 589832 | tf_op jit(solution)/shard_map/ppermute | solution.py:230
  42.5 1.0 copy-done.7
  43.5 1.0 copy-done.9
  44.5 1.0 copy-done.11
  45.5 0.9 copy-done.13
  46.5 11.2 %shard_map.95 = (bf16[256,1536]{1,0:T(8,128)(2,1)}, bf16[256,1536]{1,0:T(8,128)(2,1)}, f32[2,256,768]{2,1,0:T(8,128)S(1)}, bf16[2,128,768]{2,1,0:T(8,128)(2,1)S(...) custom-call(bf16[256,1536]{1,0:T(8,128)(2,1)S(1)} %copy-done.4, ...), custom_call_target="tpu_custom_call" | custom-call | flops 2113929216 | bytes 7864320 | tf_op jit(solution)/shard_map/pallas_call | solution.py:130
  57.7 0.7 collective-permute-start.19
  58.4 5.6 %collective-permute-start.15 = (bf16[2,128,768]{2,1,0:T(8,128)(2,1)S(1)}, bf16[2,128,768]{2,1,0:T(8,128)(2,1)S(1)}, u32[]{:S(2)}, u32[]{:S(2)}) collective-permute-start(bf16[2,128,768]{2,1,0:T(8,128)(2,1)S(1)} %get-tuple-element.55), channel_id=1, source_target_pairs={{0,8},{1,9},{2,10},{3,11},{4,12},{5,13},{6,14},{7,15},{8,0},{9,1},... | collective-permute-start | bytes 1179656 | tf_op jit(solution)/shard_map/ppermute | solution.py:241
  64.0 0.9 collective-permute-start.16
  65.2 11.2 %shard_map.96 = (bf16[256,1536]{1,0:T(8,128)(2,1)}, bf16[256,1536]{1,0:T(8,128)(2,1)}, f32[2,256,768]{2,1,0:T(8,128)S(1)}, bf16[2,128,768]{2,1,0:T(8,128)(2,1)S(...) custom-call(bf16[256,1536]{1,0:T(8,128)(2,1)S(1)} %copy-done.4, ...), custom_call_target="tpu_custom_call", output_to_operand_aliasing={{0}: (10, {}), {1}: (11, {})} | custom-call | flops 2113929216 | bytes 7864320 | tf_op jit(solution)/shard_map/pallas_call | solution.py:130
  76.9 8.6 %collective-permute-done.15.refs_0_ = bf16[2,128,768]{2,1,0:T(8,128)(2,1)S(1)} collective-permute-done((bf16[2,128,768]{2,1,0:T(8,128)(2,1)S(1)}, bf16[2,128,768]{2,1,0:T(8,128)(2,1)S(1)}, u32[]{:S(2)}, u32[]{:S(2)}) %collective-permute-start.15) | collective-permute-done | bytes 393248 | tf_op jit(solution)/shard_map/ppermute | solution.py:241
  85.5 0.9 collective-permute-start.12
  87.1 3.2 %shard_map.97 = (bf16[256,1536]{1,0:T(8,128)(2,1)}, bf16[256,1536]{1,0:T(8,128)(2,1)}) custom-call(s32[6]{0:T(128)S(1)} %pad_add_fusion.where_ref, f32[2,256,768]{2,1,0:T(8,128)S(1)} %get-tuple-element.54.own_ref, bf16[2,128,768]{2,1,0:T(8,128)(2,1)S(1)} %collective-permute-done.15.refs_0_, bf16[2,128,768]{2,1,0:T(8,128)(2,1)S(1)} %collective-permute-done.16.refs_1_, ...), custom_call_target="tpu_custom_call" | custom-call | bytes 4325376 | tf_op jit(solution)/shard_map/pallas_call | solution.py:179
  90.3 11.4 %collective-permute-done.10.refs_0_ = bf16[2,128,768]{2,1,0:T(8,128)(2,1)S(1)} collective-permute-done((bf16[2,128,768]{2,1,0:T(8,128)(2,1)S(1)}, bf16[2,128,768]{2,1,0:T(8,128)(2,1)S(1)}, u32[]{:S(2)}, u32[]{:S(2)}) %collective-permute-start.10) | collective-permute-done | bytes 393248 | tf_op jit(solution)/shard_map/ppermute | solution.py:241
  102.2 3.2 %shard_map.98 = (bf16[256,1536]{1,0:T(8,128)(2,1)}, bf16[256,1536]{1,0:T(8,128)(2,1)}) custom-call(s32[6]{0:T(128)S(1)} %pad_add_fusion.where_ref, f32[2,256,768]{2,1,0:T(8,128)S(1)} %get-tuple-element.48.own_ref, bf16[2,128,768]{2,1,0:T(8,128)(2,1)S(1)} %collective-permute-done.10.refs_0_, ...), custom_call_target="tpu_custom_call", output_to_operand_aliasing={{0}: (7, {}), {1}: (8, {})} | custom-call | bytes 4325376 | tf_op jit(solution)/shard_map/pallas_call | solution.py:179
  (58 shorter events, 7.4 us)
Async XLA Ops:
  1.4 1.1 %copy-start = (bf16[256,1536]{1,0:T(8,128)(2,1)S(1)}, bf16[256,1536]{1,0:T(8,128)(2,1)}, u32[]{:S(2)}) copy-start(bf16[256,1536]{1,0:T(8,128)(2,1)} %refs_2_.3) | copy-start | bytes 2359300
  2.5 1.1 %copy-start.2 = (bf16[256,1536]{1,0:T(8,128)(2,1)S(1)}, bf16[256,1536]{1,0:T(8,128)(2,1)}, u32[]{:S(2)}) copy-start(bf16[256,1536]{1,0:T(8,128)(2,1)} %refs_3_.3) | copy-start | bytes 2359300
  3.7 9.4 %copy-start.1 = (bf16[256,1536]{1,0:T(8,128)(2,1)S(1)}, bf16[256,1536]{1,0:T(8,128)(2,1)}, u32[]{:S(2)}) copy-start(bf16[256,1536]{1,0:T(8,128)(2,1)} %refs_2_.3) | copy-start | bytes 2359300
  3.7 9.4 %copy-start.3 = (bf16[256,1536]{1,0:T(8,128)(2,1)S(1)}, bf16[256,1536]{1,0:T(8,128)(2,1)}, u32[]{:S(2)}) copy-start(bf16[256,1536]{1,0:T(8,128)(2,1)} %refs_3_.3) | copy-start | bytes 2359300
  3.7 32.6 %copy-start.15 = (s32[1,4,2]{1,2,0:T(2,128)S(1)}, s32[1,4,2]{1,2,0:T(2,128)}, u32[]{:S(2)}) copy-start(s32[1,4,2]{1,2,0:T(2,128)} %param.10) | copy-start | bytes 100
  3.7 38.9 %copy-start.4 = (bf16[256,1536]{1,0:T(8,128)(2,1)S(1)}, bf16[256,1536]{1,0:T(8,128)(2,1)}, u32[]{:S(2)}) copy-start(bf16[256,1536]{1,0:T(8,128)(2,1)} %refs_0_.3) | copy-start | bytes 2359300
  3.7 38.9 %copy-start.5 = (bf16[256,1536]{1,0:T(8,128)(2,1)S(1)}, bf16[256,1536]{1,0:T(8,128)(2,1)}, u32[]{:S(2)}) copy-start(bf16[256,1536]{1,0:T(8,128)(2,1)} %refs_1_.3) | copy-start | bytes 2359300
  5.2 21.7 %collective-permute-start.5 = (bf16[2,128,768]{2,1,0:T(8,128)(2,1)S(1)}, bf16[2,128,768]{2,1,0:T(8,128)(2,1)S(1)}, u32[]{:S(2)}, u32[]{:S(2)}) collective-permute-start(bf16[2,128,768]{2,1,0:T(8,128)(2,1)S(1)} %get-tuple-element.39), channel_id=1, source_target_pairs={{0,8},{1,9},{2,10},{3,11},{4,12},{5,13},{6,14},{7,15},{8,0},{9,1},... | collective-permute-start | bytes 1179656 | tf_op jit(solution)/shard_map/ppermute | solution.py:230
  9.3 24.7 %collective-permute-start.6 = (bf16[2,128,768]{2,1,0:T(8,128)(2,1)S(1)}, bf16[2,128,768]{2,1,0:T(8,128)(2,1)S(1)}, u32[]{:S(2)}, u32[]{:S(2)}) collective-permute-start(bf16[2,128,768]{2,1,0:T(8,128)(2,1)S(1)} %get-tuple-element.40), channel_id=1, source_target_pairs={{0,4},{1,5},{2,6},{3,7},{4,0},{5,1},{6,2},{7,3},{8,12},{9,13},{10,... | collective-permute-start | bytes 1179656 | tf_op jit(solution)/shard_map/ppermute | solution.py:230
  10.9 24.6 %collective-permute-start.7 = (bf16[2,128,768]{2,1,0:T(8,128)(2,1)S(1)}, bf16[2,128,768]{2,1,0:T(8,128)(2,1)S(1)}, u32[]{:S(2)}, u32[]{:S(2)}) collective-permute-start(bf16[2,128,768]{2,1,0:T(8,128)(2,1)S(1)} %get-tuple-element.41), channel_id=1, source_target_pairs={{0,2},{1,3},{2,0},{3,1},{4,6},{5,7},{6,4},{7,5},{8,10},{9,11},{10,... | collective-permute-start | bytes 1179656 | tf_op jit(solution)/shard_map/ppermute | solution.py:230
  12.4 28.5 %collective-permute-start.8 = (bf16[2,192,768]{2,1,0:T(8,128)(2,1)}, bf16[2,192,768]{2,1,0:T(8,128)(2,1)}, u32[]{:S(2)}, u32[]{:S(2)}) collective-permute-start(bf16[2,192,768]{2,1,0:T(8,128)(2,1)} %get-tuple-element.42), channel_id=1, source_target_pairs={{0,1},{1,0},{2,3},{3,2},{4,5},{5,4},{6,7},{7,6},{8,9},{9,8},{10,11... | collective-permute-start | bytes 1769480 | tf_op jit(solution)/shard_map/ppermute | solution.py:230
  12.4 3.2 %collective-permute-start.9 = (bf16[2,64,768]{2,1,0:T(8,128)(2,1)S(1)}, bf16[2,64,768]{2,1,0:T(8,128)(2,1)S(1)}, u32[]{:S(2)}, u32[]{:S(2)}) collective-permute-start(bf16[2,64,768]{2,1,0:T(8,128)(2,1)S(1)} %get-tuple-element.43), channel_id=1, source_target_pairs={{0,0},{1,2},{2,1},{3,4},{4,3},{5,6},{6,5},{7,8},{8,7},{9,10},{10,9... | collective-permute-start | bytes 589832 | tf_op jit(solution)/shard_map/ppermute | solution.py:230
  16.3 48.9 %collective-permute-start.3 = (bf16[2,192,768]{2,1,0:T(8,128)(2,1)}, bf16[2,192,768]{2,1,0:T(8,128)(2,1)}, u32[]{:S(2)}, u32[]{:S(2)}) collective-permute-start(bf16[2,192,768]{2,1,0:T(8,128)(2,1)} %get-tuple-element.37), channel_id=1, source_target_pairs={{0,1},{1,0},{2,3},{3,2},{4,5},{5,4},{6,7},{7,6},{8,9},{9,8},{10,11... | collective-permute-start | bytes 1769480 | tf_op jit(solution)/shard_map/ppermute | solution.py:230
  27.7 30.6 %collective-permute-start = (bf16[2,128,768]{2,1,0:T(8,128)(2,1)}, bf16[2,128,768]{2,1,0:T(8,128)(2,1)S(1)}, u32[]{:S(2)}, u32[]{:S(2)}) collective-permute-start(bf16[2,128,768]{2,1,0:T(8,128)(2,1)} %get-tuple-element.34), channel_id=1, source_target_pairs={{0,8},{1,9},{2,10},{3,11},{4,12},{5,13},{6,14},{7,15},{8,0},{9,1},... | collective-permute-start | bytes 1179656 | tf_op jit(solution)/shard_map/ppermute | solution.py:230
  34.0 0.7 copy-start.8
  34.8 29.2 %collective-permute-start.1 = (bf16[2,128,768]{2,1,0:T(8,128)(2,1)}, bf16[2,128,768]{2,1,0:T(8,128)(2,1)}, u32[]{:S(2)}, u32[]{:S(2)}) collective-permute-start(bf16[2,128,768]{2,1,0:T(8,128)(2,1)} %get-tuple-element.35), channel_id=1, source_target_pairs={{0,4},{1,5},{2,6},{3,7},{4,0},{5,1},{6,2},{7,3},{8,12},{9,13},{10,... | collective-permute-start | bytes 1179656 | tf_op jit(solution)/shard_map/ppermute | solution.py:230
  36.2 28.6 %collective-permute-start.2 = (bf16[2,128,768]{2,1,0:T(8,128)(2,1)}, bf16[2,128,768]{2,1,0:T(8,128)(2,1)}, u32[]{:S(2)}, u32[]{:S(2)}) collective-permute-start(bf16[2,128,768]{2,1,0:T(8,128)(2,1)} %get-tuple-element.36), channel_id=1, source_target_pairs={{0,2},{1,3},{2,0},{3,1},{4,6},{5,7},{6,4},{7,5},{8,10},{9,11},{10,... | collective-permute-start | bytes 1179656 | tf_op jit(solution)/shard_map/ppermute | solution.py:230
  41.0 16.7 %collective-permute-start.4 = (bf16[2,64,768]{2,1,0:T(8,128)(2,1)}, bf16[2,64,768]{2,1,0:T(8,128)(2,1)S(1)}, u32[]{:S(2)}, u32[]{:S(2)}) collective-permute-start(bf16[2,64,768]{2,1,0:T(8,128)(2,1)} %copy-done.14), channel_id=1, source_target_pairs={{0,0},{1,2},{2,1},{3,4},{4,3},{5,6},{6,5},{7,8},{8,7},{9,10},{10,9... | collective-permute-start | bytes 589832 | tf_op jit(solution)/shard_map/ppermute | solution.py:230
  42.5 1.0 copy-start.7
  43.5 1.0 copy-start.9
  44.5 1.0 copy-start.11
  45.5 0.9 copy-start.13
  57.7 18.7 %collective-permute-start.19 = (bf16[2,64,768]{2,1,0:T(8,128)(2,1)S(1)}, bf16[2,64,768]{2,1,0:T(8,128)(2,1)S(1)}, u32[]{:S(2)}, u32[]{:S(2)}) collective-permute-start(bf16[2,64,768]{2,1,0:T(8,128)(2,1)S(1)} %get-tuple-element.59), channel_id=1, source_target_pairs={{0,0},{1,2},{2,1},{3,4},{4,3},{5,6},{6,5},{7,8},{8,7},{9,10},{10,9... | collective-permute-start | bytes 589832 | tf_op jit(solution)/shard_map/ppermute | solution.py:241
  58.4 27.1 %collective-permute-start.15 = (bf16[2,128,768]{2,1,0:T(8,128)(2,1)S(1)}, bf16[2,128,768]{2,1,0:T(8,128)(2,1)S(1)}, u32[]{:S(2)}, u32[]{:S(2)}) collective-permute-start(bf16[2,128,768]{2,1,0:T(8,128)(2,1)S(1)} %get-tuple-element.55), channel_id=1, source_target_pairs={{0,8},{1,9},{2,10},{3,11},{4,12},{5,13},{6,14},{7,15},{8,0},{9,1},... | collective-permute-start | bytes 1179656 | tf_op jit(solution)/shard_map/ppermute | solution.py:241
  64.0 21.5 %collective-permute-start.16 = (bf16[2,128,768]{2,1,0:T(8,128)(2,1)S(1)}, bf16[2,128,768]{2,1,0:T(8,128)(2,1)S(1)}, u32[]{:S(2)}, u32[]{:S(2)}) collective-permute-start(bf16[2,128,768]{2,1,0:T(8,128)(2,1)S(1)} %get-tuple-element.56), channel_id=1, source_target_pairs={{0,4},{1,5},{2,6},{3,7},{4,0},{5,1},{6,2},{7,3},{8,12},{9,13},{10,... | collective-permute-start | bytes 1179656 | tf_op jit(solution)/shard_map/ppermute | solution.py:241
  64.9 20.6 %collective-permute-start.17 = (bf16[2,128,768]{2,1,0:T(8,128)(2,1)S(1)}, bf16[2,128,768]{2,1,0:T(8,128)(2,1)S(1)}, u32[]{:S(2)}, u32[]{:S(2)}) collective-permute-start(bf16[2,128,768]{2,1,0:T(8,128)(2,1)S(1)} %get-tuple-element.57), channel_id=1, source_target_pairs={{0,2},{1,3},{2,0},{3,1},{4,6},{5,7},{6,4},{7,5},{8,10},{9,11},{10,... | collective-permute-start | bytes 1179656 | tf_op jit(solution)/shard_map/ppermute | solution.py:241
  65.2 21.2 %collective-permute-start.18 = (bf16[2,192,768]{2,1,0:T(8,128)(2,1)S(1)}, bf16[2,192,768]{2,1,0:T(8,128)(2,1)S(1)}, u32[]{:S(2)}, u32[]{:S(2)}) collective-permute-start(bf16[2,192,768]{2,1,0:T(8,128)(2,1)S(1)} %get-tuple-element.58), channel_id=1, source_target_pairs={{0,1},{1,0},{2,3},{3,2},{4,5},{5,4},{6,7},{7,6},{8,9},{9,8},{10,11... | collective-permute-start | bytes 1769480 | tf_op jit(solution)/shard_map/ppermute | solution.py:241
  76.4 25.8 %collective-permute-start.13 = (bf16[2,192,768]{2,1,0:T(8,128)(2,1)S(1)}, bf16[2,192,768]{2,1,0:T(8,128)(2,1)S(1)}, u32[]{:S(2)}, u32[]{:S(2)}) collective-permute-start(bf16[2,192,768]{2,1,0:T(8,128)(2,1)S(1)} %get-tuple-element.52), channel_id=1, source_target_pairs={{0,1},{1,0},{2,3},{3,2},{4,5},{5,4},{6,7},{7,6},{8,9},{9,8},{10,11... | collective-permute-start | bytes 1769480 | tf_op jit(solution)/shard_map/ppermute | solution.py:241
  85.5 16.2 %collective-permute-start.10 = (bf16[2,128,768]{2,1,0:T(8,128)(2,1)S(1)}, bf16[2,128,768]{2,1,0:T(8,128)(2,1)S(1)}, u32[]{:S(2)}, u32[]{:S(2)}) collective-permute-start(bf16[2,128,768]{2,1,0:T(8,128)(2,1)S(1)} %get-tuple-element.49), channel_id=1, source_target_pairs={{0,8},{1,9},{2,10},{3,11},{4,12},{5,13},{6,14},{7,15},{8,0},{9,1},... | collective-permute-start | bytes 1179656 | tf_op jit(solution)/shard_map/ppermute | solution.py:241
  85.5 16.7 %collective-permute-start.11 = (bf16[2,128,768]{2,1,0:T(8,128)(2,1)S(1)}, bf16[2,128,768]{2,1,0:T(8,128)(2,1)S(1)}, u32[]{:S(2)}, u32[]{:S(2)}) collective-permute-start(bf16[2,128,768]{2,1,0:T(8,128)(2,1)S(1)} %get-tuple-element.50), channel_id=1, source_target_pairs={{0,4},{1,5},{2,6},{3,7},{4,0},{5,1},{6,2},{7,3},{8,12},{9,13},{10,... | collective-permute-start | bytes 1179656 | tf_op jit(solution)/shard_map/ppermute | solution.py:241
  85.5 16.7 %collective-permute-start.12 = (bf16[2,128,768]{2,1,0:T(8,128)(2,1)S(1)}, bf16[2,128,768]{2,1,0:T(8,128)(2,1)S(1)}, u32[]{:S(2)}, u32[]{:S(2)}) collective-permute-start(bf16[2,128,768]{2,1,0:T(8,128)(2,1)S(1)} %get-tuple-element.51), channel_id=1, source_target_pairs={{0,2},{1,3},{2,0},{3,1},{4,6},{5,7},{6,4},{7,5},{8,10},{9,11},{10,... | collective-permute-start | bytes 1179656 | tf_op jit(solution)/shard_map/ppermute | solution.py:241
  86.4 3.9 %collective-permute-start.14 = (bf16[2,64,768]{2,1,0:T(8,128)(2,1)S(1)}, bf16[2,64,768]{2,1,0:T(8,128)(2,1)S(1)}, u32[]{:S(2)}, u32[]{:S(2)}) collective-permute-start(bf16[2,64,768]{2,1,0:T(8,128)(2,1)S(1)} %get-tuple-element.53), channel_id=1, source_target_pairs={{0,0},{1,2},{2,1},{3,4},{4,3},{5,6},{6,5},{7,8},{8,7},{9,10},{10,9... | collective-permute-start | bytes 589832 | tf_op jit(solution)/shard_map/ppermute | solution.py:241
  (4 other events, 2.8 us)
